TPU v7x, 32 devices: a whole 2x2x4 slice. The times are simulated.
32 devices in a mesh: groups: 2 (over y), ep: 4 (over z), half: 2 (over x), tp: 2 (over core).
Axes of the slice: x: 2, y: 2, z: 4, core: 2. Of those that a mesh axis runs over, the one named last changes fastest.
Arguments:
- queries: bfloat16 [512, 2048], P(('groups', 'ep', 'half'), 'tp'), parts along dimension 0, may hold values from -6 to 6
- new_keys: bfloat16 [512, 256], P(('groups', 'ep', 'half'), 'tp'), parts along dimension 0, may hold values from -4 to 4
- new_values: bfloat16 [512, 256], P(('groups', 'ep', 'half'), 'tp'), parts along dimension 0, may hold values from -4 to 4
- cache_keys: bfloat16 [512, 2, 64, 128], P(('groups', 'ep', 'half'), 'tp'), parts along dimension 0, may hold values from -4 to 4
- cache_values: bfloat16 [512, 2, 64, 128], P(('groups', 'ep', 'half'), 'tp'), parts along dimension 0, may hold values from -4 to 4
- lengths: int32 [512], P(('groups', 'ep', 'half')), parts along dimension 0, may hold values from 1 to 64, as said below
- out_weight: bfloat16 [2048, 2048], P('tp', 'half'), may hold values from -0.375 to 0.375
- residual: bfloat16 [512, 2048], P(('groups', 'ep'), 'half'), parts along dimension 0, may hold values from -5 to 5
- norm_gain: float32 [2048], P('half'), may hold values from 0.1 to 1.9
- expert_ids: int32 [512, 8], P(('groups', 'ep')), parts along dimension 0, may hold values from 0 to 63, all different within a row; in each aligned block of 64 rows (0 to 63, 64 to 127, ...) at most 12 rows name the same one
- gate_weights: float32 [512, 8], P(('groups', 'ep')), parts along dimension 0, may hold values from 0.05 to 1
- w_gate: bfloat16 [64, 768, 2048], P(('ep', 'tp'), 'half'), may hold values from -0.125 to 0.125
- w_up: bfloat16 [64, 768, 2048], P(('ep', 'tp'), 'half'), may hold values from -0.125 to 0.125
- w_down: bfloat16 [64, 768, 2048], P(('ep', 'tp'), 'half'), may hold values from -0.625 to 0.625
Outputs:
- layer_out: bfloat16 [512, 2048], P(('groups', 'ep'), ('half', 'tp')), parts along dimension 0
There are 2 independent parts, one for each index of `groups`. A program takes and returns all parts, laid end to end along the dimension named above; an argument that names none is the same for every part. Nothing has to cross between parts.
Inputs may be any that keep to these rules, and one draw needn't show every extreme that they name: `expert_ids`: in each block of 64 consecutive rows (the tokens of one index of ep) no expert is named by more than 12 rows. `lengths`: among each device's 32 requests one has 64 cached tokens.
All inputs are finite; a program needn't handle non-finite values.
Results may differ from a plain program's by a relative error of at most 0.014.
Values may be sent and summed in bfloat16 or wider, within the bound.
No kernel may reach another device: no remote copies, remote signals or barrier semaphores. Data moves between devices by JAX's collectives and lax.ppermute only.
A program may use at most 128 MiB of HBM per device.

v0:
```python
import math
import jax
import jax.numpy as jnp
from jax import lax
from jax.sharding import PartitionSpec as P

EXPERTS = 64
EPSILON = 1e-06


def attend(queries, new_keys, new_values, cache_keys, cache_values, lengths):
    requests, key_heads, context, head_size = cache_keys.shape
    sharing = queries.shape[1] // (key_heads * head_size)
    query_blocks = queries.reshape(requests, key_heads, sharing, head_size)
    score_scale = 1.0 / math.sqrt(head_size)
    scores = (
        jnp.einsum("rkgd,rkcd->rkgc", query_blocks, cache_keys, preferred_element_type=jnp.float32)
        * score_scale
    )
    own_score = (
        jnp.einsum(
            "rkgd,rkd->rkg",
            query_blocks,
            new_keys.reshape(requests, key_heads, head_size),
            preferred_element_type=jnp.float32,
        )
        * score_scale
    )
    valid = lax.iota(jnp.int32, context)[None, :] < lengths[:, None]
    scores = jnp.where(valid[:, None, None, :], scores, -1e30)
    highest = jnp.maximum(jnp.max(scores, axis=-1), own_score)
    weights = jnp.exp(scores - highest[..., None])
    own_weight = jnp.exp(own_score - highest)
    denominator = jnp.sum(weights, axis=-1) + own_weight
    probs = (weights / denominator[..., None]).astype(jnp.bfloat16)
    own_prob = (own_weight / denominator).astype(jnp.bfloat16)
    mixture = jnp.einsum("rkgc,rkcd->rkgd", probs, cache_values, preferred_element_type=jnp.float32)
    mixture = mixture + own_prob.astype(jnp.float32)[..., None] * new_values.reshape(
        requests, key_heads, 1, head_size
    ).astype(jnp.float32)
    return mixture.astype(jnp.bfloat16).reshape(requests, key_heads * sharing * head_size)


def combine_rows(returned_rows, target, gates):
    token_rows, top_count = target.shape
    safe_target = jnp.maximum(target, 0).reshape(-1)
    picked = jnp.take(returned_rows, safe_target, axis=0).reshape(
        token_rows, top_count, returned_rows.shape[1]
    )
    weighting = jnp.where(target >= 0, gates, 0.0)
    return jnp.sum(picked.astype(jnp.float32) * weighting[..., None], axis=1)


def on_device(
    queries,
    new_keys,
    new_values,
    cache_keys,
    cache_values,
    lengths,
    out_weight,
    residual,
    norm_gain,
    expert_ids,
    gate_weights,
    w_gate,
    w_up,
    w_down,
):
    attended = attend(queries, new_keys, new_values, cache_keys, cache_values, lengths)
    partial_mix = jnp.dot(
        lax.all_gather(attended, "half", axis=0, tiled=True),
        out_weight,
        preferred_element_type=jnp.float32,
    )
    mixed = lax.psum(partial_mix.astype(jnp.bfloat16), "tp").astype(jnp.float32)
    hidden = residual.astype(jnp.float32) + mixed
    squares = lax.psum(jnp.sum(hidden * hidden, axis=1), "half")
    half_width = hidden.shape[1]
    width = half_width * lax.axis_size("half")
    normed = (hidden * lax.rsqrt(squares / width + EPSILON)[:, None] * norm_gain[None, :]).astype(
        jnp.bfloat16
    )
    token_rows, top_count = expert_ids.shape
    ep_count = lax.axis_size("ep")
    tp_count = lax.axis_size("tp")
    local_experts = w_gate.shape[0]
    capacity = token_rows * top_count * 3 // (2 * EXPERTS)
    slot_count = ep_count * local_experts * capacity
    flat_ids = expert_ids.reshape(-1)
    one_hot = (flat_ids[:, None] == lax.iota(jnp.int32, EXPERTS)[None, :]).astype(jnp.int32)
    earlier = jnp.cumsum(one_hot, axis=0) - one_hot
    slot = jnp.sum(earlier * one_hot, axis=1)
    owner_ep = flat_ids // (local_experts * tp_count)
    owner_tp = flat_ids // local_experts % tp_count
    target = owner_ep * (local_experts * capacity) + flat_ids % local_experts * capacity + slot
    target = jnp.where(owner_tp == lax.axis_index("tp"), target, -1).reshape(token_rows, top_count)
    dispatch_matrix = jnp.any(
        lax.iota(jnp.int32, slot_count)[:, None, None] == target[None, :, :], axis=2
    ).astype(jnp.bfloat16)
    gates = gate_weights / jnp.sum(gate_weights, axis=1, keepdims=True)
    full_rows = lax.all_gather(normed, "half", axis=1, tiled=True)
    outgoing = jnp.dot(dispatch_matrix, full_rows, preferred_element_type=jnp.float32).astype(
        jnp.bfloat16
    )
    arrived = lax.all_to_all(
        outgoing.reshape(ep_count, local_experts, capacity, width),
        "ep",
        split_axis=0,
        concat_axis=0,
        tiled=True,
    )
    gate_part = jnp.einsum("secd,efd->secf", arrived, w_gate, preferred_element_type=jnp.float32)
    up_part = jnp.einsum("secd,efd->secf", arrived, w_up, preferred_element_type=jnp.float32)
    activation = (jax.nn.silu(gate_part) * up_part).astype(jnp.bfloat16)
    expert_out = jnp.einsum(
        "secf,efd->secd", activation, w_down, preferred_element_type=jnp.float32
    ).astype(jnp.bfloat16)
    summed = lax.psum_scatter(
        expert_out.astype(jnp.float32).astype(jnp.bfloat16), "half", scatter_dimension=3, tiled=True
    ).astype(jnp.float32)
    returned = lax.all_to_all(
        summed.reshape(ep_count, local_experts * capacity, half_width).astype(jnp.bfloat16),
        "ep",
        split_axis=0,
        concat_axis=0,
        tiled=True,
    ).astype(jnp.float32)
    term = combine_rows(returned.reshape(slot_count, half_width), target, gates)
    expert_sum = lax.psum_scatter(
        term.astype(jnp.bfloat16), "tp", scatter_dimension=1, tiled=True
    ).astype(jnp.float32)
    slice_width = expert_sum.shape[1]
    own_columns = lax.dynamic_slice_in_dim(
        hidden, lax.axis_index("tp") * slice_width, slice_width, 1
    )
    return (own_columns + expert_sum).astype(jnp.bfloat16)


def solution(mesh):
    placed = (
        P(("groups", "ep", "half"), "tp"),
        P(("groups", "ep", "half"), "tp"),
        P(("groups", "ep", "half"), "tp"),
        P(("groups", "ep", "half"), "tp", None, None),
        P(("groups", "ep", "half"), "tp", None, None),
        P(("groups", "ep", "half")),
        P("tp", "half"),
        P(("groups", "ep"), "half"),
        P("half"),
        P(("groups", "ep"), None),
        P(("groups", "ep"), None),
        P(("ep", "tp"), "half", None),
        P(("ep", "tp"), "half", None),
        P(("ep", "tp"), "half", None),
    )
    return jax.shard_map(
        on_device,
        mesh=mesh,
        in_specs=placed,
        out_specs=P(("groups", "ep"), ("half", "tp")),
        check_vma=False,
    )
```

profile of v0, /device:TPU:0, one launch (start us, length us, event | category | flops | bytes accessed | tf_op | source)
XLA Modules:
  0.0 210.5 jit_solution(17106588360139845303)
XLA Ops:
  6.5 1.0 copy.78
  7.5 0.7 iota_compare_fusion.3
  8.3 0.8 fusion.58
  9.1 1.5 fusion.76
  10.9 0.7 convert_element_type.73
  11.6 1.4 fusion.41
  13.0 6.0 %all_gather.6 = bf16[64,1024]{1,0:T(8,128)(2,1)S(1)} all-gather(bf16[32,1024]{1,0:T(8,128)(2,1)S(1)} %bitcast.97), channel_id=1, replica_groups=mesh['groups'=2,'ep'=4,'half'=2,'tp'=2] {'half'}, dimensions={0}, use_global_device_ids=true | all-gather | bytes 196608 | tf_op jit(solution)/shard_map/all_gather | solution.py:72
  19.0 1.1 convolution_convert_fusion.1
  20.5 1.2 reduce-window.6
  22.4 0.3 fusion.47
  22.7 17.3 %all-reduce.2.cloned.1.call-done = bf16[64,1024]{1,0:T(8,128)(2,1)} async-done(((bf16[64,1024]{1,0:T(8,128)(2,1)}), bf16[64,1024]{1,0:T(8,128)(2,1)}) %all-reduce.2.cloned.1.call-update) | async-done | bytes 131088 | tf_op jit(solution)/shard_map/psum | solution.py:76
  40.0 1.0 convert_add_fusion
  41.0 4.9 %psum.15 = f32[64]{0:T(128)S(1)} all-reduce(f32[64]{0:T(128)S(1)} %get-tuple-element.8), channel_id=1, replica_groups=mesh['groups'=2,'ep'=4,'half'=2,'tp'=2] {'half'}, use_global_device_ids=true, to_apply=%region_8.9 | all-reduce | flops 64 | bytes 512 | tf_op jit(solution)/shard_map/psum | solution.py:78
  46.0 1.0 multiply_convert_fusion
  47.0 5.6 %all_gather.7 = bf16[64,2048]{1,0:T(8,128)(2,1)S(1)} all-gather(bf16[64,1024]{1,0:T(8,128)(2,1)S(1)} %multiply_convert_fusion), channel_id=1, replica_groups=mesh['groups'=2,'ep'=4,'half'=2,'tp'=2] {'half'}, dimensions={1}, use_global_device_ids=true | all-gather | bytes 393216 | tf_op jit(solution)/shard_map/all_gather | solution.py:102
  52.6 1.8 convolution_convert_fusion
  54.4 3.6 %reshape.224 = bf16[4,8,12,2048]{3,2,1,0:T(8,128)(2,1)} reshape(bf16[384,2048]{1,0:T(8,128)(2,1)} %convolution_convert_fusion) | data formatting | bytes 3145728 | tf_op jit(solution)/shard_map/reshape | solution.py:107
  58.0 2.5 %copy.65 = bf16[4,8,12,2048]{3,1,2,0:T(8,128)(2,1)S(1)} copy(bf16[4,8,12,2048]{3,2,1,0:T(8,128)(2,1)} %reshape.224) | data formatting | bytes 3145728 | tf_op jit(solution)/shard_map/reshape | solution.py:107
  60.5 39.8 %all_to_all.10 = bf16[4,8,12,2048]{3,1,2,0:T(8,128)(2,1)S(1)} all-to-all(bf16[4,8,12,2048]{3,1,2,0:T(8,128)(2,1)S(1)} %copy.65), channel_id=1, replica_groups=mesh['groups'=2,'ep'=4,'half'=2,'tp'=2] {'ep'}, dimensions={0} | all-to-all | bytes 3145728 | tf_op jit(solution)/shard_map/all_to_all | solution.py:106
  100.2 1.1 copy-done.1
  101.4 8.7 %fusion.16 = f32[4,8,12,384]{3,2,0,1:T(8,128)S(1)} fusion(bf16[8,384,2048]{2,1,0:T(8,128)(2,1)} %param.25, bf16[4,8,12,2048]{3,1,2,0:T(8,128)(2,1)S(1)} %all_to_all.10), kind=kOutput, calls=%fused_computation.15 | convolution fusion | flops 603979776 | bytes 14745600 | tf_op jit(solution)/shard_map/secd,efd->secf/dot_general | solution.py:113
  110.1 18.4 %fusion.9 = bf16[4,8,12,2048]{3,2,0,1:T(8,128)(2,1)} fusion(bf16[8,384,2048]{2,1,0:T(8,128)(2,1)} %param.27, bf16[8,384,2048]{2,1,0:T(8,128)(2,1)} %param.26, bf16[4,8,12,2048]{3,1,2,0:T(8,128)(2,1)} %copy-done.1, f32[4,8,12,384]{3,2,0,1:T(8,128)S(1)} %fusion.16), kind=kOutput, calls=%fused_computation.9 | convolution fusion | flops 1209630720 | bytes 28901376 | tf_op jit(solution)/shard_map/secf,efd->secd/dot_general | solution.py:116
  128.5 31.1 %reduce-scatter.3.cloned.1.call-done = bf16[4,8,12,1024]{3,2,0,1:T(8,128)(2,1)} async-done(((bf16[4,8,12,2048]{3,2,0,1:T(8,128)(2,1)}), bf16[4,8,12,1024]{3,2,0,1:T(8,128)(2,1)}) %reduce-scatter.3.cloned.1.call-update) | async-done | bytes 786448 | tf_op jit(solution)/shard_map/reduce_scatter | solution.py:119
  159.6 1.8 copy.68
  161.4 1.1 copy.69
  162.5 4.6 %all-to-all-start.1 = ((bf16[4,96,1024]{2,1,0:T(8,128)(2,1)}), bf16[4,96,1024]{2,1,0:T(8,128)(2,1)S(1)}, u32[]{:S(2)}, u32[]{:S(2)}) async-start(bf16[4,96,1024]{2,1,0:T(8,128)(2,1)} %copy.69), calls=%async_computation.2 | async-start | bytes 1572864 | tf_op jit(solution)/shard_map/all_to_all | solution.py:122
  167.6 19.5 %all-to-all-done.1 = bf16[4,96,1024]{2,1,0:T(8,128)(2,1)S(1)} async-done(((bf16[4,96,1024]{2,1,0:T(8,128)(2,1)}), bf16[4,96,1024]{2,1,0:T(8,128)(2,1)S(1)}, u32[]{:S(2)}, u32[]{:S(2)}) %all-to-all-start.1) | async-done | bytes 786464 | tf_op jit(solution)/shard_map/all_to_all | solution.py:122
  187.1 1.4 bitcast_convert_fusion
  188.5 5.1 %gather_fusion = f32[512,1024]{1,0:T(8,128)} fusion(f32[384,1024]{1,0:T(8,128)} %bitcast_convert_fusion, s32[1024]{0:T(1024)S(1)} %pad_clamp_fusion), kind=kCustom, calls=%fused_computation | custom fusion | bytes 4196352 | tf_op jit(solution)/shard_map/jit(_take)/gather | solution.py:47
  193.5 3.0 %fusion.15 = bf16[64,1024]{1,0:T(8,128)(2,1)} fusion(f32[512,1024]{1,0:T(8,128)} %gather_fusion, f32[64,8]{1,0:T(8,128)S(1)} %copy.71, pred[64,8]{1,0:T(8,128)(4,1)S(1)} %copy.63), kind=kLoop, calls=%fused_computation.14 | loop fusion | flops 1507328 | bytes 2230784 | tf_op jit(solution)/shard_map/reduce_sum | solution.py:51
  196.6 5.9 %reduce-scatter.5.cloned.1.call-done = bf16[64,512]{1,0:T(8,128)(2,1)} async-done(((bf16[64,1024]{1,0:T(8,128)(2,1)}), bf16[64,512]{1,0:T(8,128)(2,1)}) %reduce-scatter.5.cloned.1.call-update) | async-done | bytes 65552 | tf_op jit(solution)/shard_map/reduce_scatter | solution.py:130
  202.5 1.5 add_convert_fusion
  (43 shorter events, 1.7 us)
Async XLA Ops:
  6.5 12.4 %copy-start = (bf16[1024,1024]{1,0:T(8,128)(2,1)S(1)}, bf16[1024,1024]{1,0:T(8,128)(2,1)}, u32[]{:S(2)}) copy-start(bf16[1024,1024]{1,0:T(8,128)(2,1)} %param.20) | copy-start | bytes 6291460
  6.5 33.5 %all-reduce.2.cloned.1.call-start = ((), (), s32[]{:S(2)}) async-start(), calls=%async_computation.4 | async-start | bytes 262144 | tf_op jit(solution)/shard_map/psum | solution.py:76
  10.6 9.5 %copy-start.3 = (s32[64,8]{0,1:T(8,128)S(1)}, s32[64,8]{0,1:T(8,128)}, u32[]{:S(2)}) copy-start(s32[64,8]{0,1:T(8,128)} %param.23) | copy-start | bytes 6148
  12.9 27.1 %copy-start.2 = (bf16[64,1024]{1,0:T(8,128)(2,1)S(1)}, bf16[64,1024]{1,0:T(8,128)(2,1)}, u32[]{:S(2)}) copy-start(bf16[64,1024]{1,0:T(8,128)(2,1)} %param.21) | copy-start | bytes 393220
  13.0 33.0 %copy-start.5 = (f32[1024]{0:T(1024)S(1)}, f32[1024]{0:T(1024)}, u32[]{:S(2)}) copy-start(f32[1024]{0:T(1024)} %param.22) | copy-start | bytes 12292
  20.1 139.5 %reduce-scatter.3.cloned.1.call-start = ((), (), s32[]{:S(2)}) async-start(), calls=%async_computation.5 | async-start | bytes 3145728 | tf_op jit(solution)/shard_map/reduce_scatter | solution.py:119
  100.2 1.1 copy-start.1
  128.5 38.8 %copy-start.4 = (f32[64,8]{0,1:T(8,128)S(1)}, f32[64,8]{0,1:T(8,128)}, u32[]{:S(2)}) copy-start(f32[64,8]{0,1:T(8,128)} %param.24) | copy-start | bytes 6148
  162.5 24.5 %all-to-all-start.1 = ((bf16[4,96,1024]{2,1,0:T(8,128)(2,1)}), bf16[4,96,1024]{2,1,0:T(8,128)(2,1)S(1)}, u32[]{:S(2)}, u32[]{:S(2)}) async-start(bf16[4,96,1024]{2,1,0:T(8,128)(2,1)} %copy.69), calls=%async_computation.2 | async-start | bytes 1572864 | tf_op jit(solution)/shard_map/all_to_all | solution.py:122
  167.1 35.3 %reduce-scatter.5.cloned.1.call-start = ((), (), s32[]{:S(2)}) async-start(), calls=%async_computation.6 | async-start | bytes 196608 | tf_op jit(solution)/shard_map/reduce_scatter | solution.py:130
Sparse Core Ops, SparseCore 0:
  20.2 19.6 all-reduce.1
  128.6 30.9 reduce-scatter.2
  196.7 5.7 reduce-scatter.4
where the time goes:
time: 211 us; the launch traced here: 210 us
  waiting for transfers between devices  73.9 us (35%)
  blocking collectives  56.3 us (27%)
  matrix products  33.7 us (16%)
  local copies, waits for them, and re-layouts  17.4 us (8%)
  between operations  13.3 us (6%)
  other arithmetic  11.3 us (5%)
  starting transfers between devices  4.62 us (2%)
    all_to_all x1, blocking collectives, on_device(): lax.all_to_all(outgoing.reshape(ep_count, local_experts, capacity, width)...  39.8 us
    reduce_scatter x1, waiting for transfers between devices, on_device(): lax.psum_scatter(expert_out.astype(jnp.float32).astype(jnp.bfloat16), 'ha...  31.1 us
    all_to_all x1, waiting for transfers between devices, on_device(): lax.all_to_all(summed.reshape(ep_count, local_experts * capacity, half_wi...  19.5 us
    dot_general x1, matrix products, on_device(): jnp.einsum('secf,efd->secd', activation, w_down, preferred_element_type=j...  18.4 us
    psum x1, waiting for transfers between devices, on_device(): mixed = lax.psum(partial_mix.astype(jnp.bfloat16), 'tp').astype(jnp.float32)  17.3 us
    dot_general x1, matrix products, on_device(): jnp.einsum('secd,efd->secf', arrived, w_gate, preferred_element_type=jnp....  8.68 us
    reshape x2, local copies, waits for them, and re-layouts, on_device(): outgoing.reshape(ep_count, local_experts, capacity, width)  6.06 us
    all_gather x1, blocking collectives, on_device(): lax.all_gather(attended, 'half', axis=0, tiled=True)  6 us
  transfers between devices with their start and end apart: 4, of which 4 were waited for; matrix products, arithmetic and copies ran while one was open for 1% of the time, Pallas kernels for 0%

commit v1 on v0

--- a/solution.py
+++ b/solution.py
@@ -73,7 +73,9 @@
         out_weight,
         preferred_element_type=jnp.float32,
     )
-    mixed = lax.psum(partial_mix.astype(jnp.bfloat16), "tp").astype(jnp.float32)
+    mixed = jnp.sum(lax.all_gather(partial_mix.astype(jnp.bfloat16), "tp"), axis=0).astype(
+        jnp.float32
+    )
     hidden = residual.astype(jnp.float32) + mixed
     squares = lax.psum(jnp.sum(hidden * hidden, axis=1), "half")
     half_width = hidden.shape[1]

time: 211 us -> 195 us (0.924)
  waiting for transfers between devices: 73.9 us -> 56.6 us
  blocking collectives: 56.3 us -> 58.6 us
    psum x1 -> x0, waiting for transfers between devices: 17.3 us -> none  [on_device(): mixed = lax.psum(partial_mix.astype(jnp.bfloat16), 'tp').astype(jnp.float32)]
  transfers between devices with their start and end apart: 4 -> 3, of which waited for: 4 -> 3; matrix products, arithmetic and copies ran while one was open for 1% -> 0% of each run, Pallas kernels for 0% -> 0%
where the time goes in v1:
time: 195 us; the launch traced here: 194 us
  blocking collectives  58.6 us (30%)
  waiting for transfers between devices  56.6 us (29%)
  matrix products  33 us (17%)
  local copies, waits for them, and re-layouts  18 us (9%)
  between operations  13.6 us (7%)
  other arithmetic  9.58 us (5%)
  starting transfers between devices  4.59 us (2%)
    all_to_all x1, blocking collectives, on_device(): lax.all_to_all(outgoing.reshape(ep_count, local_experts, capacity, width)...  40.2 us
    reduce_scatter x1, waiting for transfers between devices, on_device(): lax.psum_scatter(expert_out.astype(jnp.float32).astype(jnp.bfloat16), 'ha...  31.2 us
    all_to_all x1, waiting for transfers between devices, on_device(): lax.all_to_all(summed.reshape(ep_count, local_experts * capacity, half_wi...  19.5 us
    dot_general x1, matrix products, on_device(): jnp.einsum('secf,efd->secd', activation, w_down, preferred_element_type=j...  18.4 us
    dot_general x1, matrix products, on_device(): jnp.einsum('secd,efd->secf', arrived, w_gate, preferred_element_type=jnp....  8.69 us
    reshape x2, local copies, waits for them, and re-layouts, on_device(): outgoing.reshape(ep_count, local_experts, capacity, width)  6.06 us
    reduce_scatter x1, waiting for transfers between devices, on_device(): lax.psum_scatter(term.astype(jnp.bfloat16), 'tp', scatter_dimension=1, ti...  5.87 us
    all_gather x1, blocking collectives, on_device(): lax.all_gather(attended, 'half', axis=0, tiled=True)  5.86 us
  transfers between devices with their start and end apart: 3, of which 3 were waited for; matrix products, arithmetic and copies ran while one was open for 0% of the time, Pallas kernels for 0%

profile of v1, /device:TPU:0, one launch (start us, length us, event | category | flops | bytes accessed | tf_op | source)
XLA Modules:
  0.0 194.1 jit_solution(10395389772654285416)
XLA Ops:
  6.5 0.9 copy.59
  7.6 0.9 copy.78
  8.5 0.7 iota_compare_fusion.3
  9.2 0.8 fusion.58
  10.1 1.5 fusion.76
  11.8 0.7 convert_element_type.75
  12.5 1.4 fusion.41
  13.9 5.9 %all_gather.12 = bf16[64,1024]{1,0:T(8,128)(2,1)S(1)} all-gather(bf16[32,1024]{1,0:T(8,128)(2,1)S(1)} %bitcast.99), channel_id=1, replica_groups=mesh['groups'=2,'ep'=4,'half'=2,'tp'=2] {'half'}, dimensions={0}, use_global_device_ids=true | all-gather | bytes 196608 | tf_op jit(solution)/shard_map/all_gather | solution.py:72
  19.8 0.5 convolution_convert_fusion.1
  20.3 2.0 %all-gather = bf16[128,1024]{1,0:T(8,128)(2,1)S(1)} all-gather(bf16[64,1024]{1,0:T(8,128)(2,1)S(1)} %convolution_convert_fusion.1), channel_id=2, replica_groups=mesh['groups'=2,'ep'=4,'half'=2,'tp'=2] {'tp'}, dimensions={0}, use_global_device_ids=true | all-gather | bytes 393216 | tf_op jit(solution)/shard_map/all_gather | solution.py:76
  22.5 4.9 %psum.7 = f32[64]{0:T(128)S(1)} all-reduce(f32[64]{0:T(128)S(1)} %get-tuple-element.8), channel_id=1, replica_groups=mesh['groups'=2,'ep'=4,'half'=2,'tp'=2] {'half'}, use_global_device_ids=true, to_apply=%region_8.9 | all-reduce | flops 64 | bytes 512 | tf_op jit(solution)/shard_map/psum | solution.py:80
  27.6 5.6 %all_gather.15 = bf16[64,2048]{1,0:T(8,128)(2,1)S(1)} all-gather(bf16[64,1024]{1,0:T(8,128)(2,1)S(1)} %multiply_convert_fusion), channel_id=1, replica_groups=mesh['groups'=2,'ep'=4,'half'=2,'tp'=2] {'half'}, dimensions={1}, use_global_device_ids=true | all-gather | bytes 393216 | tf_op jit(solution)/shard_map/all_gather | solution.py:104
  33.2 1.2 reduce-window.6
  34.4 0.2 slice_reduce_fusion
  35.1 0.3 fusion.47
  35.4 1.8 convolution_convert_fusion
  37.2 3.6 %reshape.224 = bf16[4,8,12,2048]{3,2,1,0:T(8,128)(2,1)} reshape(bf16[384,2048]{1,0:T(8,128)(2,1)} %convolution_convert_fusion) | data formatting | bytes 3145728 | tf_op jit(solution)/shard_map/reshape | solution.py:109
  40.8 2.5 %copy.65 = bf16[4,8,12,2048]{3,1,2,0:T(8,128)(2,1)S(1)} copy(bf16[4,8,12,2048]{3,2,1,0:T(8,128)(2,1)} %reshape.224) | data formatting | bytes 3145728 | tf_op jit(solution)/shard_map/reshape | solution.py:109
  43.2 40.2 %all_to_all.10 = bf16[4,8,12,2048]{3,1,2,0:T(8,128)(2,1)S(1)} all-to-all(bf16[4,8,12,2048]{3,1,2,0:T(8,128)(2,1)S(1)} %copy.65), channel_id=1, replica_groups=mesh['groups'=2,'ep'=4,'half'=2,'tp'=2] {'ep'}, dimensions={0} | all-to-all | bytes 3145728 | tf_op jit(solution)/shard_map/all_to_all | solution.py:108
  83.4 1.1 copy-done.1
  84.6 8.7 %fusion.16 = f32[4,8,12,384]{3,2,0,1:T(8,128)S(1)} fusion(bf16[8,384,2048]{2,1,0:T(8,128)(2,1)} %param.25, bf16[4,8,12,2048]{3,1,2,0:T(8,128)(2,1)S(1)} %all_to_all.10), kind=kOutput, calls=%fused_computation.15 | convolution fusion | flops 603979776 | bytes 14745600 | tf_op jit(solution)/shard_map/secd,efd->secf/dot_general | solution.py:115
  93.3 18.4 %fusion.9 = bf16[4,8,12,2048]{3,2,0,1:T(8,128)(2,1)} fusion(bf16[8,384,2048]{2,1,0:T(8,128)(2,1)} %param.27, bf16[8,384,2048]{2,1,0:T(8,128)(2,1)} %param.26, bf16[4,8,12,2048]{3,1,2,0:T(8,128)(2,1)} %copy-done.1, f32[4,8,12,384]{3,2,0,1:T(8,128)S(1)} %fusion.16), kind=kOutput, calls=%fused_computation.9 | convolution fusion | flops 1209630720 | bytes 28901376 | tf_op jit(solution)/shard_map/secf,efd->secd/dot_general | solution.py:118
  111.7 31.2 %reduce-scatter.3.cloned.1.call-done = bf16[4,8,12,1024]{3,2,0,1:T(8,128)(2,1)} async-done(((bf16[4,8,12,2048]{3,2,0,1:T(8,128)(2,1)}), bf16[4,8,12,1024]{3,2,0,1:T(8,128)(2,1)}) %reduce-scatter.3.cloned.1.call-update) | async-done | bytes 786448 | tf_op jit(solution)/shard_map/reduce_scatter | solution.py:121
  142.9 1.8 copy.68
  144.7 1.1 copy.69
  145.8 4.6 %all-to-all-start.1 = ((bf16[4,96,1024]{2,1,0:T(8,128)(2,1)}), bf16[4,96,1024]{2,1,0:T(8,128)(2,1)S(1)}, u32[]{:S(2)}, u32[]{:S(2)}) async-start(bf16[4,96,1024]{2,1,0:T(8,128)(2,1)} %copy.69), calls=%async_computation.2 | async-start | bytes 1572864 | tf_op jit(solution)/shard_map/all_to_all | solution.py:124
  150.9 19.5 %all-to-all-done.1 = bf16[4,96,1024]{2,1,0:T(8,128)(2,1)S(1)} async-done(((bf16[4,96,1024]{2,1,0:T(8,128)(2,1)}), bf16[4,96,1024]{2,1,0:T(8,128)(2,1)S(1)}, u32[]{:S(2)}, u32[]{:S(2)}) %all-to-all-start.1) | async-done | bytes 786464 | tf_op jit(solution)/shard_map/all_to_all | solution.py:124
  170.4 1.4 bitcast_convert_fusion
  171.7 5.1 %gather_fusion = f32[512,1024]{1,0:T(8,128)} fusion(f32[384,1024]{1,0:T(8,128)} %bitcast_convert_fusion, s32[1024]{0:T(1024)S(1)} %pad_clamp_fusion), kind=kCustom, calls=%fused_computation | custom fusion | bytes 4196352 | tf_op jit(solution)/shard_map/jit(_take)/gather | solution.py:47
  176.8 3.0 %fusion.15 = bf16[64,1024]{1,0:T(8,128)(2,1)} fusion(f32[512,1024]{1,0:T(8,128)} %gather_fusion, f32[64,8]{1,0:T(8,128)S(1)} %copy.71, pred[64,8]{1,0:T(8,128)(4,1)S(1)} %copy.63), kind=kLoop, calls=%fused_computation.14 | loop fusion | flops 1507328 | bytes 2230784 | tf_op jit(solution)/shard_map/reduce_sum | solution.py:51
  179.9 5.9 %reduce-scatter.5.cloned.1.call-done = bf16[64,512]{1,0:T(8,128)(2,1)} async-done(((bf16[64,1024]{1,0:T(8,128)(2,1)}), bf16[64,512]{1,0:T(8,128)(2,1)}) %reduce-scatter.5.cloned.1.call-update) | async-done | bytes 65552 | tf_op jit(solution)/shard_map/reduce_scatter | solution.py:132
  185.7 1.5 add_convert_fusion
  (42 shorter events, 1.6 us)
Async XLA Ops:
  6.5 13.3 %copy-start = (bf16[1024,1024]{1,0:T(8,128)(2,1)S(1)}, bf16[1024,1024]{1,0:T(8,128)(2,1)}, u32[]{:S(2)}) copy-start(bf16[1024,1024]{1,0:T(8,128)(2,1)} %param.20) | copy-start | bytes 6291460
  6.5 136.3 %reduce-scatter.3.cloned.1.call-start = ((), (), s32[]{:S(2)}) async-start(), calls=%async_computation.4 | async-start | bytes 3145728 | tf_op jit(solution)/shard_map/reduce_scatter | solution.py:121
  12.5 9.8 %copy-start.2 = (bf16[64,1024]{1,0:T(8,128)(2,1)S(1)}, bf16[64,1024]{1,0:T(8,128)(2,1)}, u32[]{:S(2)}) copy-start(bf16[64,1024]{1,0:T(8,128)(2,1)} %param.21) | copy-start | bytes 393220
  13.9 13.5 %copy-start.5 = (f32[1024]{0:T(1024)S(1)}, f32[1024]{0:T(1024)}, u32[]{:S(2)}) copy-start(f32[1024]{0:T(1024)} %param.22) | copy-start | bytes 12292
  19.8 15.2 %copy-start.3 = (s32[64,8]{0,1:T(8,128)S(1)}, s32[64,8]{0,1:T(8,128)}, u32[]{:S(2)}) copy-start(s32[64,8]{0,1:T(8,128)} %param.23) | copy-start | bytes 6148
  83.4 1.1 copy-start.1
  111.6 39.0 %copy-start.4 = (f32[64,8]{0,1:T(8,128)S(1)}, f32[64,8]{0,1:T(8,128)}, u32[]{:S(2)}) copy-start(f32[64,8]{0,1:T(8,128)} %param.24) | copy-start | bytes 6148
  145.8 24.5 %all-to-all-start.1 = ((bf16[4,96,1024]{2,1,0:T(8,128)(2,1)}), bf16[4,96,1024]{2,1,0:T(8,128)(2,1)S(1)}, u32[]{:S(2)}, u32[]{:S(2)}) async-start(bf16[4,96,1024]{2,1,0:T(8,128)(2,1)} %copy.69), calls=%async_computation.2 | async-start | bytes 1572864 | tf_op jit(solution)/shard_map/all_to_all | solution.py:124
  150.4 35.3 %reduce-scatter.5.cloned.1.call-start = ((), (), s32[]{:S(2)}) async-start(), calls=%async_computation.5 | async-start | bytes 196608 | tf_op jit(solution)/shard_map/reduce_scatter | solution.py:132
Sparse Core Ops, SparseCore 0:
  111.8 31.0 reduce-scatter.2
  180.0 5.7 reduce-scatter.4
